TPU v7x, 32 devices: a whole 2x2x4 slice. The times are simulated.
32 devices in a mesh: ctx: 8 (over z, x), tp: 4 (over y, core).
Axes of the slice: x: 2, y: 2, z: 4, core: 2. Of those that a mesh axis runs over, the one named last changes fastest.
Arguments:
- q_nope: bfloat16 [8, 128, 128], P('ctx', 'tp'), may hold values from -6 to 6
- q_rope: bfloat16 [8, 128, 64], P('ctx', 'tp'), may hold values from -256 to 256
- w_uk: bfloat16 [128, 128, 512], P('tp'), may hold values from -0.5 to 0.5
- w_uv: bfloat16 [128, 512, 128], P('tp'), may hold values from -3 to 3
- w_out: bfloat16 [16384, 7168], P('tp', 'ctx'), may hold values from -0.046875 to 0.046875
- prefix_cache: bfloat16 [32768, 576], P('ctx'), may hold values from -6 to 6
- block_table: int32 [512], P('ctx'), may hold values from 0 to 511, each once
- prefix_len: int32 [8], replicated, may hold values from 8192 to 32768
- suffix_cache: bfloat16 [8, 256, 576], P('ctx'), may hold values from -12 to 12
- suffix_len: int32 [8], P('ctx'), may hold values from 2 to 256
Outputs:
- layer_out: bfloat16 [8, 7168], P('tp', 'ctx')
Inputs may be any that keep to these rules, and one draw needn't show every extreme that they name: A permutation: slots b * 64 to b * 64 + 63 of prefix_cache hold prefix positions block_table[b] * 64 onwards.
All inputs are finite; a program needn't handle non-finite values.
Results may differ from a plain program's by a relative error of at most 0.0078.
Values may be sent and summed in bfloat16 or wider, within the bound.
A program may use at most 64 MiB of HBM per device.

v0:
```python
import jax
import jax.numpy as jnp
from jax import lax
from jax.sharding import PartitionSpec as P

LAT = 512
ROPE = 64
NOPE = 128
BLOCK = 64
masked_value = -1e30


def partial_stats(scores, visible, values, pattern):
    row_peak = jnp.max(jnp.where(visible, scores, masked_value), axis=2)
    weights = jnp.where(visible, jnp.exp(scores - row_peak[:, :, None]), 0.0).astype(jnp.bfloat16)
    row_mass = jnp.sum(weights, axis=2, dtype=jnp.float32)
    row_weighted = jnp.einsum(pattern, weights, values, preferred_element_type=jnp.float32)
    return (row_peak, row_mass, row_weighted)


def value_project(latent, value_weight):
    return jnp.einsum("rhc,hcv->rhv", latent, value_weight, precision=lax.Precision.HIGHEST)


def on_device(
    q_nope,
    q_rope,
    w_uk,
    w_uv,
    w_out,
    prefix_cache,
    block_table,
    prefix_len,
    suffix_cache,
    suffix_len,
):
    softmax_scale = (NOPE + ROPE) ** (-0.5)
    q_latent = jnp.einsum("rhn,hnc->rhc", q_nope, w_uk, preferred_element_type=jnp.float32).astype(
        jnp.bfloat16
    )
    own_queries = jnp.concatenate([q_latent, q_rope], axis=2)
    all_queries = lax.all_gather(own_queries, "ctx", axis=0, tiled=True)
    ctx_count = lax.axis_size("ctx")
    own_count = own_queries.shape[0]
    value_weight = w_uv.astype(jnp.float32)
    positions = (
        block_table[:, None] * BLOCK + jnp.arange(BLOCK, dtype=jnp.int32)[None, :]
    ).reshape(-1)
    visible = (positions[None, :] < prefix_len[:, None])[:, None, :]
    scores = (
        jnp.einsum("rhc,tc->rht", all_queries, prefix_cache, preferred_element_type=jnp.float32)
        * softmax_scale
    )
    row_peak, row_mass, row_weighted = partial_stats(
        scores, visible, prefix_cache[:, :LAT], "rht,tc->rhc"
    )
    suffix_scores = (
        jnp.einsum("rhc,rtc->rht", own_queries, suffix_cache, preferred_element_type=jnp.float32)
        * softmax_scale
    )
    suffix_slots = jnp.arange(suffix_cache.shape[1], dtype=jnp.int32)
    suffix_visible = (suffix_slots[None, :] < suffix_len[:, None])[:, None, :]
    tail_peak, tail_mass, tail_weighted = partial_stats(
        suffix_scores, suffix_visible, suffix_cache[:, :, :LAT], "rht,rtc->rhc"
    )

    def by_owner(values):
        return values.reshape((ctx_count, own_count) + values.shape[1:])

    got_peak, got_mass, got_weighted = (
        lax.all_to_all(by_owner(row_peak), "ctx", split_axis=0, concat_axis=0, tiled=True),
        lax.all_to_all(by_owner(row_mass), "ctx", split_axis=0, concat_axis=0, tiled=True),
        lax.all_to_all(by_owner(row_weighted), "ctx", split_axis=0, concat_axis=0, tiled=True),
    )
    highest = jnp.maximum(jnp.max(got_peak, axis=0), tail_peak)
    factors = jnp.exp(got_peak - highest[None])
    tail_factor = jnp.exp(tail_peak - highest)
    total_mass = jnp.sum(factors * got_mass, axis=0) + tail_factor * tail_mass
    total_weighted = (
        jnp.sum(factors[..., None] * got_weighted, axis=0) + tail_factor[:, :, None] * tail_weighted
    )
    head_values = value_project(total_weighted / total_mass[:, :, None], value_weight).astype(
        jnp.bfloat16
    )
    flat_values = head_values.reshape(own_count, -1)
    every_value = lax.all_gather(flat_values, "ctx", axis=0, tiled=True)
    return lax.psum_scatter(
        jnp.dot(every_value, w_out, preferred_element_type=jnp.float32),
        "tp",
        scatter_dimension=0,
        tiled=True,
    ).astype(jnp.bfloat16)


def solution(mesh):
    placed = (
        P("ctx", "tp", None),
        P("ctx", "tp", None),
        P("tp", None, None),
        P("tp", None, None),
        P("tp", "ctx"),
        P("ctx", None),
        P("ctx"),
        P(),
        P("ctx", None, None),
        P("ctx"),
    )
    return jax.shard_map(
        on_device, mesh=mesh, in_specs=placed, out_specs=P("tp", "ctx"), check_vma=False
    )
```

profile of v0, /device:TPU:0, one launch (start us, length us, event | category | flops | bytes accessed | tf_op | source)
XLA Modules:
  0.0 129.5 jit_solution(10840114998855403633)
XLA Ops:
  0.0 0.0 copy-start
  0.0 0.7 broadcast_multiply_fusion
  0.7 0.1 iota_add_fusion
  0.8 0.1 add.38
  0.9 0.0 copy-done
  0.9 3.0 %fusion.20 = bf16[32,1,512]{2,1,0:T(2,128)(2,1)S(1)} fusion(bf16[32,128,512]{2,1,0:T(8,128)(2,1)} %param.12, bf16[32,128,1]{1,0,2:T(8,128)(2,1)S(1)} %bitcast.55), kind=kOutput, calls=%fused_computation.32 | convolution fusion | flops 4194304 | bytes 4235264 | tf_op jit(solution)/shard_map/rhn,hnc->rhc/dot_general | solution.py:38
  3.9 0.0 copy-done.3
  3.9 32.7 %all_gather.6 = bf16[8,32,576]{2,1,0:T(8,128)(2,1)S(1)} all-gather(bf16[1,32,576]{2,1,0:T(8,128)(2,1)S(1)} %pad_maximum_fusion), channel_id=1, replica_groups=mesh['ctx'=8,'tp'=4] {'ctx'}, dimensions={0}, use_global_device_ids=true | all-gather | bytes 331776 | tf_op jit(solution)/shard_map/all_gather | solution.py:42
  36.6 0.0 copy-done.4
  36.6 0.1 broadcast_compare_fusion
  36.7 0.0 copy-done.5
  36.7 2.7 %select_reduce_fusion = (f32[8,32]{1,0:T(8,128)}, f32[8,32,4096]{2,1,0:T(8,128)S(1)}) fusion(pred[8,4096]{1,0:T(8,128)(4,1)S(1)} %broadcast_compare_fusion, bf16[8,32,576]{2,1,0:T(8,128)(2,1)S(1)} %all_gather.6, bf16[4096,576]{0,1:T(8,128)(2,1)S(1)} %copy-done.5), kind=kOutput, calls=%fused_computation.7 | convolution fusion | flops 1211105024 | bytes 9241600 | tf_op jit(solution)/shard_map/rhc,tc->rht/dot_general | solution.py:51
  39.4 1.9 %copy-done.1 = f32[8,32,4096]{2,1,0:T(8,128)} copy-done((f32[8,32,4096]{2,1,0:T(8,128)}, f32[8,32,4096]{2,1,0:T(8,128)S(1)}, u32[]{:S(2)}) %copy-start.1) | copy-done | bytes 4194328
  41.3 1.7 %convert_reduce_fusion = f32[8,32]{1,0:T(8,128)S(1)} fusion(f32[8,32,4096]{2,1,0:T(8,128)S(1)} %get-tuple-element.10, f32[8,32]{1,0:T(8,128)} %get-tuple-element.9, pred[8,4096]{1,0:T(8,128)(4,1)S(1)} %broadcast_compare_fusion), kind=kLoop, calls=%fused_computation.4 | loop fusion | flops 5242624 | bytes 4229120 | tf_op jit(solution)/shard_map/reduce_sum | solution.py:16
  43.0 11.8 %all_to_all.15 = f32[8,1,32]{2,1,0:T(1,128)S(1)} all-to-all(f32[8,1,32]{2,1,0:T(1,128)S(1)} %bitcast.60), channel_id=1, replica_groups=mesh['ctx'=8,'tp'=4] {'ctx'}, dimensions={0} | all-to-all | bytes 2048 | tf_op jit(solution)/shard_map/all_to_all | solution.py:72
  54.9 3.2 %all-to-all-start = ((f32[8,1,32]{2,1,0:T(1,128)}), f32[8,1,32]{2,1,0:T(1,128)S(1)}, u32[]{:S(2)}, u32[]{:S(2)}) async-start(f32[8,1,32]{2,1,0:T(1,128)} %bitcast.5), calls=%async_computation | async-start | bytes 8192 | tf_op jit(solution)/shard_map/all_to_all | solution.py:71
  58.1 0.0 copy-start.6
  58.1 0.0 copy-start.2
  58.1 5.6 %fusion.4 = f32[8,1,32,512]{3,2,1,0:T(8,128)} fusion(bf16[4096,576]{0,1:T(8,128)(2,1)} %param.15, f32[8,32,4096]{2,1,0:T(8,128)} %copy-done.1, f32[8,32]{1,0:T(8,128)} %get-tuple-element.9, pred[8,4096]{1,0:T(8,128)(4,1)S(1)} %broadcast_compare_fusion), kind=kOutput, calls=%fused_computation.8 | convolution fusion | flops 1076887552 | bytes 8949760 | tf_op jit(solution)/shard_map/rht,tc->rhc/dot_general | solution.py:17
  63.7 0.8 all-to-all-done
  64.5 5.1 %all-to-all-start.1 = ((f32[8,1,32,512]{3,2,1,0:T(8,128)}), f32[8,1,32,512]{3,2,1,0:T(8,128)S(1)}, u32[]{:S(2)}, u32[]{:S(2)}) async-start(f32[8,1,32,512]{3,2,1,0:T(8,128)} %fusion.4), calls=%async_computation.1 | async-start | bytes 1048576 | tf_op jit(solution)/shard_map/all_to_all | solution.py:73
  70.3 0.7 dynamic-slice
  71.7 0.3 select_reduce_fusion.1
  72.0 0.2 convert_reduce_fusion.1
  72.2 7.8 %all-to-all-done.1 = f32[8,1,32,512]{3,2,1,0:T(8,128)S(1)} async-done(((f32[8,1,32,512]{3,2,1,0:T(8,128)}), f32[8,1,32,512]{3,2,1,0:T(8,128)S(1)}, u32[]{:S(2)}, u32[]{:S(2)}) %all-to-all-start.1) | async-done | bytes 524320 | tf_op jit(solution)/shard_map/all_to_all | solution.py:73
  80.0 0.1 multiply_reduce_fusion
  80.1 0.2 fusion.9
  80.3 3.5 %fusion.16 = f32[32,1,128]{2,1,0:T(1,128)S(1)} fusion(bf16[32,512,128]{2,1,0:T(8,128)(2,1)} %param.13, f32[32,512,1]{1,0,2:T(8,128)S(1)} %fusion.9), kind=kOutput, calls=%fused_computation.22 | convolution fusion | flops 25165824 | bytes 4276224 | tf_op jit(solution)/shard_map/rhc,hcv->rhv/dot_general | solution.py:22
  83.9 30.5 %all-gather = bf16[8,1,4096]{2,1,0:T(2,128)(2,1)S(1)} all-gather(bf16[1,1,4096]{2,1,0:T(2,128)(2,1)S(1)} %reshape.166), channel_id=1, replica_groups=mesh['ctx'=8,'tp'=4] {'ctx'}, dimensions={0}, use_global_device_ids=true | all-gather | bytes 73728 | tf_op jit(solution)/shard_map/all_gather | solution.py:86
  114.4 4.1 %fusion.13 = f32[8,896]{1,0:T(8,128)S(1)} fusion(bf16[4096,896]{1,0:T(8,128)(2,1)} %param.14, bf16[8,1,4096]{2,1,0:T(2,128)(2,1)S(1)} %all-gather), kind=kOutput, calls=%fused_computation.18 | convolution fusion | flops 58720256 | bytes 7434240 | tf_op jit(solution)/shard_map/dot_general | solution.py:88
  118.6 10.3 %all-reduce = bf16[8,896]{1,0:T(8,128)(2,1)S(1)} all-reduce(f32[8,896]{1,0:T(8,128)S(1)} %fusion.13), channel_id=2, replica_groups=mesh['ctx'=8,'tp'=4] {'tp'}, use_global_device_ids=true, to_apply=%region_7.8.clone | all-reduce | flops 7168 | bytes 43008
  128.9 0.6 dynamic-slice_convert_fusion
  (15 shorter events, 0.1 us)
Async XLA Ops:
  0.0 0.9 copy-start
  0.0 3.9 %copy-start.3 = (bf16[1,32,64]{2,1,0:T(8,128)(2,1)S(1)}, bf16[1,32,64]{2,1,0:T(8,128)(2,1)}, u32[]{:S(2)}) copy-start(bf16[1,32,64]{2,1,0:T(8,128)(2,1)} %param.11) | copy-start | bytes 12292
  0.0 36.6 %copy-start.4 = (s32[8]{0:T(128)S(1)}, s32[8]{0:T(128)}, u32[]{:S(2)}) copy-start(s32[8]{0:T(128)} %param.17) | copy-start | bytes 100
  0.9 35.8 %copy-start.5 = (bf16[4096,576]{0,1:T(8,128)(2,1)S(1)}, bf16[4096,576]{0,1:T(8,128)(2,1)}, u32[]{:S(2)}) copy-start(bf16[4096,576]{0,1:T(8,128)(2,1)} %param.15) | copy-start | bytes 14155780
  39.4 1.9 %copy-start.1 = (f32[8,32,4096]{2,1,0:T(8,128)}, f32[8,32,4096]{2,1,0:T(8,128)S(1)}, u32[]{:S(2)}) copy-start(f32[8,32,4096]{2,1,0:T(8,128)S(1)} %get-tuple-element.10) | copy-start | bytes 12582916
  54.9 9.7 %all-to-all-start = ((f32[8,1,32]{2,1,0:T(1,128)}), f32[8,1,32]{2,1,0:T(1,128)S(1)}, u32[]{:S(2)}, u32[]{:S(2)}) async-start(f32[8,1,32]{2,1,0:T(1,128)} %bitcast.5), calls=%async_computation | async-start | bytes 8192 | tf_op jit(solution)/shard_map/all_to_all | solution.py:71
  58.1 12.2 %copy-start.6 = (u32[32]{0:T(128)S(1)}, u32[32]{0:T(128)}, u32[]{:S(2)}) copy-start(u32[32]{0:T(128)} %constant.17) | copy-start | bytes 388
  58.1 13.6 %copy-start.2 = (bf16[1,256,576]{1,2,0:T(8,128)(2,1)S(1)}, bf16[1,256,576]{1,2,0:T(8,128)(2,1)}, u32[]{:S(2)}) copy-start(bf16[1,256,576]{1,2,0:T(8,128)(2,1)} %param.18) | copy-start | bytes 884740
  64.5 15.5 %all-to-all-start.1 = ((f32[8,1,32,512]{3,2,1,0:T(8,128)}), f32[8,1,32,512]{3,2,1,0:T(8,128)S(1)}, u32[]{:S(2)}, u32[]{:S(2)}) async-start(f32[8,1,32,512]{3,2,1,0:T(8,128)} %fusion.4), calls=%async_computation.1 | async-start | bytes 1048576 | tf_op jit(solution)/shard_map/all_to_all | solution.py:73
where the time goes:
time: 130 us; the launch traced here: 129 us
  blocking collectives  85.4 us (66%)
  matrix products  19.4 us (15%)
  waiting for transfers between devices  8.58 us (7%)
  starting transfers between devices  8.34 us (6%)
  local copies, waits for them, and re-layouts  3.31 us (3%)
  other arithmetic  3 us (2%)
  between operations  1.49 us (1%)
    all_gather x1, blocking collectives, on_device(): all_queries = lax.all_gather(own_queries, 'ctx', axis=0, tiled=True)  32.7 us
    all_gather x1, blocking collectives, on_device(): every_value = lax.all_gather(flat_values, 'ctx', axis=0, tiled=True)  30.5 us
    all_to_all x1, blocking collectives, on_device(): lax.all_to_all(by_owner(row_mass), 'ctx', split_axis=0, concat_axis=0, ti...  11.8 us
    unnamed x1, blocking collectives  10.3 us
    all_to_all x1, waiting for transfers between devices, on_device(): lax.all_to_all(by_owner(row_weighted), 'ctx', split_axis=0, concat_axis=0...  7.78 us
    dot_general x2, matrix products, partial_stats(): jnp.einsum(pattern, weights, values, preferred_element_type=jnp.float32)  5.81 us
    all_to_all x1, starting transfers between devices, on_device(): lax.all_to_all(by_owner(row_weighted), 'ctx', split_axis=0, concat_axis=0...  5.12 us
    dot_general x1, matrix products, on_device(): jnp.dot(every_value, w_out, preferred_element_type=jnp.float32)  4.14 us
  transfers between devices with their start and end apart: 2, of which 2 were waited for; matrix products, arithmetic and copies ran while one was open for 5% of the time, Pallas kernels for 0%

commit v1 on v0

--- a/solution.py
+++ b/solution.py
@@ -83,7 +83,14 @@
         jnp.bfloat16
     )
     flat_values = head_values.reshape(own_count, -1)
-    every_value = lax.all_gather(flat_values, "ctx", axis=0, tiled=True)
+    size = lax.axis_size("ctx")
+    forward = [(i, (i + 1) % size) for i in range(size)]
+    parts = [flat_values]
+    for far in range(1, size):
+        parts = [lax.ppermute(parts[0], "ctx", forward), *parts]
+    full = jnp.concatenate(parts, axis=0)
+    turn = (lax.axis_index("ctx") + 1) * parts[-1].shape[0]
+    every_value = jnp.roll(full, turn, axis=0)
     return lax.psum_scatter(
         jnp.dot(every_value, w_out, preferred_element_type=jnp.float32),
         "tp",

time: 130 us -> 143 us (1.10)
  waiting for transfers between devices: 8.58 us -> 54.8 us
  blocking collectives: 85.4 us -> 43 us
  starting transfers between devices: 8.34 us -> 15.8 us
  other arithmetic: 3 us -> 5.07 us
  matrix products: 19.4 us -> 21.2 us
  local copies, waits for them, and re-layouts: 3.31 us -> 1.69 us
    ppermute x0 -> x7, waiting for transfers between devices: none -> 42.2 us  [on_device(): parts = [lax.ppermute(parts[0], 'ctx', forward), *parts]]
    all_gather x1 -> x0, blocking collectives: 30.5 us -> none  [on_device(): every_value = lax.all_gather(flat_values, 'ctx', axis=0, tiled=True)]
    all_to_all x1 -> x0, blocking collectives: 11.8 us -> none  [on_device(): lax.all_to_all(by_owner(row_mass), 'ctx', split_axis=0, concat_axis=0, ti...]
    all_to_all x0 -> x1, starting transfers between devices: none -> 3.33 us  [on_device(): lax.all_to_all(by_owner(row_mass), 'ctx', split_axis=0, concat_axis=0, ti...]
    all_to_all x1, starting transfers between devices: 3.22 us -> 5.56 us  [on_device(): lax.all_to_all(by_owner(row_peak), 'ctx', split_axis=0, concat_axis=0, ti...]
    reduce_sum x2, other arithmetic: 1.93 us -> 4.01 us  [partial_stats(): row_mass = jnp.sum(weights, axis=2, dtype=jnp.float32)]
    unnamed x16 -> x14, local copies, waits for them, and re-layouts: 2.63 us -> 0.62 us
    all_to_all x1, waiting for transfers between devices: 0.79 us -> 2.68 us  [on_device(): lax.all_to_all(by_owner(row_peak), 'ctx', split_axis=0, concat_axis=0, ti...]
  transfers between devices with their start and end apart: 2 -> 10, of which waited for: 2 -> 10; matrix products, arithmetic and copies ran while one was open for 5% -> 7% of each run, Pallas kernels for 0% -> 0%
where the time goes in v1:
time: 143 us
  waiting for transfers between devices  54.8 us (38%)
  blocking collectives  43 us (30%)
  matrix products  21.2 us (15%)
  starting transfers between devices  15.8 us (11%)
  other arithmetic  5.07 us (4%)
  local copies, waits for them, and re-layouts  1.69 us (1%)
  between operations  1.44 us (1%)
    ppermute x7, waiting for transfers between devices, on_device(): parts = [lax.ppermute(parts[0], 'ctx', forward), *parts]  42.2 us
    all_gather x1, blocking collectives, on_device(): all_queries = lax.all_gather(own_queries, 'ctx', axis=0, tiled=True)  32.7 us
    unnamed x1, blocking collectives  10.3 us
    all_to_all x1, waiting for transfers between devices, on_device(): lax.all_to_all(by_owner(row_weighted), 'ctx', split_axis=0, concat_axis=0...  9.06 us
    dot_general x2, matrix products, partial_stats(): jnp.einsum(pattern, weights, values, preferred_element_type=jnp.float32)  5.81 us
    all_to_all x1, starting transfers between devices, on_device(): lax.all_to_all(by_owner(row_peak), 'ctx', split_axis=0, concat_axis=0, ti...  5.56 us
    all_to_all x1, starting transfers between devices, on_device(): lax.all_to_all(by_owner(row_weighted), 'ctx', split_axis=0, concat_axis=0...  5.25 us
    dot_general x1, matrix products, on_device(): jnp.einsum('rhc,tc->rht', all_queries, prefix_cache, preferred_element_ty...  4.53 us
  transfers between devices with their start and end apart: 10, of which 10 were waited for; matrix products, arithmetic and copies ran while one was open for 7% of the time, Pallas kernels for 0%

profile of v1, /device:TPU:0, one launch (start us, length us, event | category | flops | bytes accessed | tf_op | source)
XLA Modules:
  0.0 143.0 jit_solution(10552600363920445594)
XLA Ops:
  0.0 0.7 broadcast_multiply_fusion
  0.8 0.1 add.51
  0.9 3.0 %fusion.19 = bf16[32,1,512]{2,1,0:T(2,128)(2,1)S(1)} fusion(bf16[32,128,512]{2,1,0:T(8,128)(2,1)} %param.12, bf16[32,128,1]{1,0,2:T(8,128)(2,1)S(1)} %bitcast.58), kind=kOutput, calls=%fused_computation.32 | convolution fusion | flops 4194304 | bytes 4235264 | tf_op jit(solution)/shard_map/rhn,hnc->rhc/dot_general | solution.py:38
  3.9 32.7 %all_gather.3 = bf16[8,32,576]{2,1,0:T(8,128)(2,1)S(1)} all-gather(bf16[1,32,576]{2,1,0:T(8,128)(2,1)S(1)} %pad_maximum_fusion), channel_id=1, replica_groups=mesh['ctx'=8,'tp'=4] {'ctx'}, dimensions={0}, use_global_device_ids=true | all-gather | bytes 331776 | tf_op jit(solution)/shard_map/all_gather | solution.py:42
  36.6 0.1 broadcast_compare_fusion
  36.7 4.5 %select_reduce_fusion = (f32[8,32]{1,0:T(8,128)}, f32[8,32,4096]{2,1,0:T(8,128)}) fusion(pred[8,4096]{1,0:T(8,128)(4,1)S(1)} %broadcast_compare_fusion, bf16[8,32,576]{2,1,0:T(8,128)(2,1)S(1)} %all_gather.3, bf16[4096,576]{0,1:T(8,128)(2,1)S(1)} %copy-done.4), kind=kOutput, calls=%fused_computation.7 | convolution fusion | flops 1211105024 | bytes 9241600 | tf_op jit(solution)/shard_map/rhc,tc->rht/dot_general | solution.py:51
  41.2 5.6 %all-to-all-start = ((f32[8,1,32]{2,1,0:T(1,128)}), f32[8,1,32]{2,1,0:T(1,128)S(1)}, u32[]{:S(2)}, u32[]{:S(2)}) async-start(f32[8,1,32]{2,1,0:T(1,128)} %bitcast.5), calls=%async_computation | async-start | bytes 8192 | tf_op jit(solution)/shard_map/all_to_all | solution.py:71
  46.8 3.8 %convert_reduce_fusion = f32[8,32]{1,0:T(8,128)} fusion(f32[8,32,4096]{2,1,0:T(8,128)} %get-tuple-element.10, f32[8,32]{1,0:T(8,128)} %get-tuple-element.9, pred[8,4096]{1,0:T(8,128)(4,1)S(1)} %broadcast_compare_fusion), kind=kLoop, calls=%fused_computation.4 | loop fusion | flops 5242624 | bytes 4229120 | tf_op jit(solution)/shard_map/reduce_sum | solution.py:16
  50.6 2.7 %all-to-all-done = f32[8,1,32]{2,1,0:T(1,128)S(1)} async-done(((f32[8,1,32]{2,1,0:T(1,128)}), f32[8,1,32]{2,1,0:T(1,128)S(1)}, u32[]{:S(2)}, u32[]{:S(2)}) %all-to-all-start) | async-done | bytes 1056 | tf_op jit(solution)/shard_map/all_to_all | solution.py:71
  53.2 3.3 %all-to-all-start.2 = ((f32[8,1,32]{2,1,0:T(1,128)}), f32[8,1,32]{2,1,0:T(1,128)S(1)}, u32[]{:S(2)}, u32[]{:S(2)}) async-start(f32[8,1,32]{2,1,0:T(1,128)} %bitcast.14), calls=%async_computation.2 | async-start | bytes 8192 | tf_op jit(solution)/shard_map/all_to_all | solution.py:72
  56.6 5.6 %fusion.4 = f32[8,1,32,512]{3,2,1,0:T(8,128)} fusion(bf16[4096,576]{0,1:T(8,128)(2,1)} %param.15, f32[8,32,4096]{2,1,0:T(8,128)} %get-tuple-element.10, f32[8,32]{1,0:T(8,128)} %get-tuple-element.9, pred[8,4096]{1,0:T(8,128)(4,1)S(1)} %broadcast_compare_fusion), kind=kOutput, calls=%fused_computation.8 | convolution fusion | flops 1076887552 | bytes 8949760 | tf_op jit(solution)/shard_map/rht,tc->rhc/dot_general | solution.py:17
  62.2 0.9 all-to-all-done.2
  63.1 5.3 %all-to-all-start.1 = ((f32[8,1,32,512]{3,2,1,0:T(8,128)}), f32[8,1,32,512]{3,2,1,0:T(8,128)S(1)}, u32[]{:S(2)}, u32[]{:S(2)}) async-start(f32[8,1,32,512]{3,2,1,0:T(8,128)} %fusion.4), calls=%async_computation.1 | async-start | bytes 1048576 | tf_op jit(solution)/shard_map/all_to_all | solution.py:73
  69.0 0.3 select_reduce_fusion.1
  69.3 0.2 convert_reduce_fusion.1
  69.5 9.1 %all-to-all-done.1 = f32[8,1,32,512]{3,2,1,0:T(8,128)S(1)} async-done(((f32[8,1,32,512]{3,2,1,0:T(8,128)}), f32[8,1,32,512]{3,2,1,0:T(8,128)S(1)}, u32[]{:S(2)}, u32[]{:S(2)}) %all-to-all-start.1) | async-done | bytes 524320 | tf_op jit(solution)/shard_map/all_to_all | solution.py:73
  78.6 0.1 multiply_reduce_fusion
  78.7 0.2 fusion.9
  78.9 3.5 %fusion.13 = f32[32,1,128]{2,1,0:T(1,128)S(1)} fusion(bf16[32,512,128]{2,1,0:T(8,128)(2,1)} %param.13, f32[32,512,1]{1,0,2:T(8,128)S(1)} %fusion.9), kind=kOutput, calls=%fused_computation.19 | convolution fusion | flops 25165824 | bytes 4276224 | tf_op jit(solution)/shard_map/rhc,hcv->rhv/dot_general | solution.py:22
  82.5 1.7 %collective-permute-start = (bf16[1,4096]{1,0:T(2,128)(2,1)S(1)}, bf16[1,4096]{1,0:T(2,128)(2,1)S(1)}, u32[]{:S(2)}, u32[]{:S(2)}) collective-permute-start(bf16[1,4096]{1,0:T(2,128)(2,1)S(1)} %bitcast.61), channel_id=1, source_target_pairs={{0,4},{4,8},{8,12},{12,16},{16,20},{20,24},{24,28},{28,0},{1,5},{5... | collective-permute-start | bytes 24584 | tf_op jit(solution)/shard_map/ppermute | solution.py:90
  84.2 4.8 %collective-permute-done = bf16[1,4096]{1,0:T(2,128)(2,1)S(1)} collective-permute-done((bf16[1,4096]{1,0:T(2,128)(2,1)S(1)}, bf16[1,4096]{1,0:T(2,128)(2,1)S(1)}, u32[]{:S(2)}, u32[]{:S(2)}) %collective-permute-start) | collective-permute-done | bytes 8224 | tf_op jit(solution)/shard_map/ppermute | solution.py:90
  88.9 6.4 %collective-permute-done.1 = bf16[1,4096]{1,0:T(2,128)(2,1)S(1)} collective-permute-done((bf16[1,4096]{1,0:T(2,128)(2,1)S(1)}, bf16[1,4096]{1,0:T(2,128)(2,1)S(1)}, u32[]{:S(2)}, u32[]{:S(2)}) %collective-permute-start.1) | collective-permute-done | bytes 8224 | tf_op jit(solution)/shard_map/ppermute | solution.py:90
  95.4 6.4 %collective-permute-done.2 = bf16[1,4096]{1,0:T(2,128)(2,1)S(1)} collective-permute-done((bf16[1,4096]{1,0:T(2,128)(2,1)S(1)}, bf16[1,4096]{1,0:T(2,128)(2,1)S(1)}, u32[]{:S(2)}, u32[]{:S(2)}) %collective-permute-start.2) | collective-permute-done | bytes 8224 | tf_op jit(solution)/shard_map/ppermute | solution.py:90
  101.8 6.4 %collective-permute-done.3 = bf16[1,4096]{1,0:T(2,128)(2,1)S(1)} collective-permute-done((bf16[1,4096]{1,0:T(2,128)(2,1)S(1)}, bf16[1,4096]{1,0:T(2,128)(2,1)S(1)}, u32[]{:S(2)}, u32[]{:S(2)}) %collective-permute-start.3) | collective-permute-done | bytes 8224 | tf_op jit(solution)/shard_map/ppermute | solution.py:90
  108.3 6.4 %collective-permute-done.4 = bf16[1,4096]{1,0:T(2,128)(2,1)S(1)} collective-permute-done((bf16[1,4096]{1,0:T(2,128)(2,1)S(1)}, bf16[1,4096]{1,0:T(2,128)(2,1)S(1)}, u32[]{:S(2)}, u32[]{:S(2)}) %collective-permute-start.4) | collective-permute-done | bytes 8224 | tf_op jit(solution)/shard_map/ppermute | solution.py:90
  114.7 6.4 %collective-permute-done.5 = bf16[1,4096]{1,0:T(2,128)(2,1)S(1)} collective-permute-done((bf16[1,4096]{1,0:T(2,128)(2,1)S(1)}, bf16[1,4096]{1,0:T(2,128)(2,1)S(1)}, u32[]{:S(2)}, u32[]{:S(2)}) %collective-permute-start.5) | collective-permute-done | bytes 8224 | tf_op jit(solution)/shard_map/ppermute | solution.py:90
  121.1 0.6 dynamic-slice
  122.4 5.2 %collective-permute-done.6 = bf16[1,4096]{1,0:T(2,128)(2,1)S(1)} collective-permute-done((bf16[1,4096]{1,0:T(2,128)(2,1)S(1)}, bf16[1,4096]{1,0:T(2,128)(2,1)S(1)}, u32[]{:S(2)}, u32[]{:S(2)}) %collective-permute-start.6) | collective-permute-done | bytes 8224 | tf_op jit(solution)/shard_map/ppermute | solution.py:90
  127.6 0.4 concatenate.10
  128.0 4.1 %fusion.15 = f32[8,896]{1,0:T(8,128)S(1)} fusion(bf16[4096,896]{1,0:T(8,128)(2,1)} %param.14, bf16[16,4096]{1,0:T(8,128)(2,1)S(1)} %concatenate.10, s32[]{:T(128)S(6)} %select_n.34), kind=kOutput, calls=%fused_computation.21 | convolution fusion | flops 58720256 | bytes 7434244 | tf_op jit(solution)/shard_map/dot_general | solution.py:95
  132.1 10.3 %all-reduce = bf16[8,896]{1,0:T(8,128)(2,1)S(1)} all-reduce(f32[8,896]{1,0:T(8,128)S(1)} %fusion.15), channel_id=2, replica_groups=mesh['ctx'=8,'tp'=4] {'tp'}, use_global_device_ids=true, to_apply=%region_7.8.clone | all-reduce | flops 7168 | bytes 43008
  142.4 0.6 dynamic-slice_convert_fusion
  (28 shorter events, 0.2 us)
Async XLA Ops:
  0.0 0.9 copy-start
  0.0 3.9 %copy-start.2 = (bf16[1,32,64]{2,1,0:T(8,128)(2,1)S(1)}, bf16[1,32,64]{2,1,0:T(8,128)(2,1)}, u32[]{:S(2)}) copy-start(bf16[1,32,64]{2,1,0:T(8,128)(2,1)} %param.11) | copy-start | bytes 12292
  0.0 36.6 %copy-start.3 = (s32[8]{0:T(128)S(1)}, s32[8]{0:T(128)}, u32[]{:S(2)}) copy-start(s32[8]{0:T(128)} %param.17) | copy-start | bytes 100
  0.9 35.8 %copy-start.4 = (bf16[4096,576]{0,1:T(8,128)(2,1)S(1)}, bf16[4096,576]{0,1:T(8,128)(2,1)}, u32[]{:S(2)}) copy-start(bf16[4096,576]{0,1:T(8,128)(2,1)} %param.15) | copy-start | bytes 14155780
  41.2 12.0 %all-to-all-start = ((f32[8,1,32]{2,1,0:T(1,128)}), f32[8,1,32]{2,1,0:T(1,128)S(1)}, u32[]{:S(2)}, u32[]{:S(2)}) async-start(f32[8,1,32]{2,1,0:T(1,128)} %bitcast.5), calls=%async_computation | async-start | bytes 8192 | tf_op jit(solution)/shard_map/all_to_all | solution.py:71
  53.2 9.8 %all-to-all-start.2 = ((f32[8,1,32]{2,1,0:T(1,128)}), f32[8,1,32]{2,1,0:T(1,128)S(1)}, u32[]{:S(2)}, u32[]{:S(2)}) async-start(f32[8,1,32]{2,1,0:T(1,128)} %bitcast.14), calls=%async_computation.2 | async-start | bytes 8192 | tf_op jit(solution)/shard_map/all_to_all | solution.py:72
  56.6 12.4 %copy-start.1 = (bf16[1,256,576]{1,2,0:T(8,128)(2,1)S(1)}, bf16[1,256,576]{1,2,0:T(8,128)(2,1)}, u32[]{:S(2)}) copy-start(bf16[1,256,576]{1,2,0:T(8,128)(2,1)} %param.18) | copy-start | bytes 884740
  62.2 58.9 %copy-start.5 = (u32[32]{0:T(128)S(1)}, u32[32]{0:T(128)}, u32[]{:S(2)}) copy-start(u32[32]{0:T(128)} %constant.47) | copy-start | bytes 388
  63.1 15.5 %all-to-all-start.1 = ((f32[8,1,32,512]{3,2,1,0:T(8,128)}), f32[8,1,32,512]{3,2,1,0:T(8,128)S(1)}, u32[]{:S(2)}, u32[]{:S(2)}) async-start(f32[8,1,32,512]{3,2,1,0:T(8,128)} %fusion.4), calls=%async_computation.1 | async-start | bytes 1048576 | tf_op jit(solution)/shard_map/all_to_all | solution.py:73
  82.5 6.5 %collective-permute-start = (bf16[1,4096]{1,0:T(2,128)(2,1)S(1)}, bf16[1,4096]{1,0:T(2,128)(2,1)S(1)}, u32[]{:S(2)}, u32[]{:S(2)}) collective-permute-start(bf16[1,4096]{1,0:T(2,128)(2,1)S(1)} %bitcast.61), channel_id=1, source_target_pairs={{0,4},{4,8},{8,12},{12,16},{16,20},{20,24},{24,28},{28,0},{1,5},{5... | collective-permute-start | bytes 24584 | tf_op jit(solution)/shard_map/ppermute | solution.py:90
  88.9 6.4 %collective-permute-start.1 = (bf16[1,4096]{1,0:T(2,128)(2,1)S(1)}, bf16[1,4096]{1,0:T(2,128)(2,1)S(1)}, u32[]{:S(2)}, u32[]{:S(2)}) collective-permute-start(bf16[1,4096]{1,0:T(2,128)(2,1)S(1)} %collective-permute-done), channel_id=1, source_target_pairs={{0,4},{4,8},{8,12},{12,16},{16,20},{20,24},{24,28},{28,0},{1,5},{5... | collective-permute-start | bytes 24584 | tf_op jit(solution)/shard_map/ppermute | solution.py:90
  95.4 6.4 %collective-permute-start.2 = (bf16[1,4096]{1,0:T(2,128)(2,1)S(1)}, bf16[1,4096]{1,0:T(2,128)(2,1)S(1)}, u32[]{:S(2)}, u32[]{:S(2)}) collective-permute-start(bf16[1,4096]{1,0:T(2,128)(2,1)S(1)} %collective-permute-done.1), channel_id=1, source_target_pairs={{0,4},{4,8},{8,12},{12,16},{16,20},{20,24},{24,28},{28,0},{1,5},{5... | collective-permute-start | bytes 24584 | tf_op jit(solution)/shard_map/ppermute | solution.py:90
  101.8 6.4 %collective-permute-start.3 = (bf16[1,4096]{1,0:T(2,128)(2,1)S(1)}, bf16[1,4096]{1,0:T(2,128)(2,1)S(1)}, u32[]{:S(2)}, u32[]{:S(2)}) collective-permute-start(bf16[1,4096]{1,0:T(2,128)(2,1)S(1)} %collective-permute-done.2), channel_id=1, source_target_pairs={{0,4},{4,8},{8,12},{12,16},{16,20},{20,24},{24,28},{28,0},{1,5},{5... | collective-permute-start | bytes 24584 | tf_op jit(solution)/shard_map/ppermute | solution.py:90
  108.3 6.4 %collective-permute-start.4 = (bf16[1,4096]{1,0:T(2,128)(2,1)S(1)}, bf16[1,4096]{1,0:T(2,128)(2,1)S(1)}, u32[]{:S(2)}, u32[]{:S(2)}) collective-permute-start(bf16[1,4096]{1,0:T(2,128)(2,1)S(1)} %collective-permute-done.3), channel_id=1, source_target_pairs={{0,4},{4,8},{8,12},{12,16},{16,20},{20,24},{24,28},{28,0},{1,5},{5... | collective-permute-start | bytes 24584 | tf_op jit(solution)/shard_map/ppermute | solution.py:90
  114.7 6.4 %collective-permute-start.5 = (bf16[1,4096]{1,0:T(2,128)(2,1)S(1)}, bf16[1,4096]{1,0:T(2,128)(2,1)S(1)}, u32[]{:S(2)}, u32[]{:S(2)}) collective-permute-start(bf16[1,4096]{1,0:T(2,128)(2,1)S(1)} %collective-permute-done.4), channel_id=1, source_target_pairs={{0,4},{4,8},{8,12},{12,16},{16,20},{20,24},{24,28},{28,0},{1,5},{5... | collective-permute-start | bytes 24584 | tf_op jit(solution)/shard_map/ppermute | solution.py:90
  121.1 6.4 %collective-permute-start.6 = (bf16[1,4096]{1,0:T(2,128)(2,1)S(1)}, bf16[1,4096]{1,0:T(2,128)(2,1)S(1)}, u32[]{:S(2)}, u32[]{:S(2)}) collective-permute-start(bf16[1,4096]{1,0:T(2,128)(2,1)S(1)} %collective-permute-done.5), channel_id=1, source_target_pairs={{0,4},{4,8},{8,12},{12,16},{16,20},{20,24},{24,28},{28,0},{1,5},{5... | collective-permute-start | bytes 24584 | tf_op jit(solution)/shard_map/ppermute | solution.py:90
